TPU v7x, 512 devices: a whole 4x4x16 slice. The times are simulated.
512 devices in a mesh: probe: 16 (over y, x), space: 32 (over z, core).
Axes of the slice: x: 4, y: 4, z: 16, core: 2. Of those that a mesh axis runs over, the one named last changes fastest.
Arguments:
- probes: float32 [128, 131072], P('probe', 'space'), may hold values from -6 to 6
- sensitivity: float32 [8, 8, 65536], P(None, None, 'space'), may hold values from -2.1 to 2.1
- obs_weight: float32 [8, 65536], P(None, 'space'), may hold values from 0.5 to 4
- prior_weight: float32 [131072], P('space'), may hold values from 0.2 to 2
- connectivity: int32 [8, 65536], P(None, 'space'), may hold values from 0 to 4351, as said below
Outputs:
- basis: float32 [128, 131072], P('probe', 'space')
- factor: float32 [128, 128], replicated
Inputs may be any that keep to these rules, and one draw needn't show every extreme that they name: Each column holds 8 distinct numbers. For an element of the block of device d of space (columns d * 2048 to (d + 1) * 2048 - 1), connectivity + d * 4096 - 128 is an existing node, and the values 0 and 4351 are both named wherever those nodes exist.
All inputs are finite; a program needn't handle non-finite values.
Results may differ from a plain program's by a relative error of at most 0.0003.
Values sent between devices are 32-bit elements; how exact they have to be, the bound alone decides.
No kernel may reach another device: no remote copies, remote signals or barrier semaphores. Data moves between devices by JAX's collectives and lax.ppermute only.
A program may use at most 64 MiB of HBM per device.

v0:
```python
import math
import jax
import jax.numpy as jnp
from jax import lax
from jax.sharding import PartitionSpec as P

HALO = 128
highest = lax.Precision.HIGHEST


def extended_2(block, sides, width):
    for axis, dim in sides:
        count = lax.axis_size(axis)
        forward = [(i, i + 1) for i in range(count - 1)]
        backward = [(target, source) for source, target in forward]
        low = lax.ppermute(
            lax.slice_in_dim(block, block.shape[dim] - width, None, axis=dim), axis, forward
        )
        high = lax.ppermute(lax.slice_in_dim(block, 0, width, axis=dim), axis, backward)
        block = jnp.concatenate([low, block, high], axis=dim)
    return block


def shifted(block, axis, distance):
    devices = range(lax.axis_size(axis))
    route = [(i - distance, i) for i in devices if i - distance in devices]
    return lax.ppermute(block, axis, route)


def element_images(extended, sensitivity, obs_weight, local):
    gathered = extended[:, local]
    gauss_count = sensitivity.shape[0]
    corner_count = sensitivity.shape[1]
    observed = []
    for gauss in range(gauss_count):
        total = gathered[:, 0, :] * sensitivity[gauss, 0][None, :]
        for corner in range(1, corner_count):
            total = total + gathered[:, corner, :] * sensitivity[gauss, corner][None, :]
        observed.append(total * obs_weight[gauss][None, :])
    pulled = []
    for corner in range(corner_count):
        total = observed[0] * sensitivity[0, corner][None, :]
        for gauss in range(1, gauss_count):
            total = total + observed[gauss] * sensitivity[gauss, corner][None, :]
        pulled.append(total)
    pulled = jnp.stack(pulled, axis=1)
    return jnp.zeros(extended.shape, jnp.float32).at[:, local].add(pulled)


def gram_over_space(partial_value):
    return lax.psum(partial_value, "space")


def orthonormal(rows, reduce_gram):
    gram_first = reduce_gram(
        jnp.dot(rows, rows.T, precision=highest, preferred_element_type=jnp.float32)
    )
    lower_first = jnp.linalg.cholesky(gram_first)
    basis_first = lax.linalg.triangular_solve(lower_first, rows, left_side=True, lower=True)
    gram_second = reduce_gram(
        jnp.dot(basis_first, basis_first.T, precision=highest, preferred_element_type=jnp.float32)
    )
    lower_second = jnp.linalg.cholesky(gram_second)
    basis = lax.linalg.triangular_solve(lower_second, basis_first, left_side=True, lower=True)
    factor = jnp.dot(
        lower_first, lower_second, precision=highest, preferred_element_type=jnp.float32
    ).T
    return (basis, factor)


def on_device(probes, sensitivity, obs_weight, prior_weight, connectivity):
    node_count = probes.shape[1]
    probe_count = probes.shape[0]
    extended = extended_2(probes, (("space", 1),), HALO)
    summed = element_images(extended, sensitivity, obs_weight, connectivity)
    lower_rim = shifted(summed[:, :HALO], "space", -1)
    upper_rim = shifted(summed[:, HALO + node_count :], "space", 1)
    images = summed[:, HALO : HALO + node_count] + prior_weight[None, :] * probes
    images = images.at[:, node_count - HALO :].add(lower_rim)
    images = images.at[:, :HALO].add(upper_rim)
    scale = math.sqrt(float(node_count * lax.axis_size("space")))
    whole = lax.all_gather(images, "probe", axis=0, tiled=True)
    basis, factor = orthonormal(whole, gram_over_space)
    basis = lax.dynamic_slice_in_dim(basis, lax.axis_index("probe") * probe_count, probe_count, 0)
    return (basis * scale, factor / scale)


def solution(mesh):
    return jax.shard_map(
        on_device,
        mesh=mesh,
        in_specs=(
            P("probe", "space"),
            P(None, None, "space"),
            P(None, "space"),
            P("space"),
            P(None, "space"),
        ),
        out_specs=(P("probe", "space"), P()),
        check_vma=False,
    )
```

profile of v0, /device:TPU:1, one launch (start us, length us, event | category | flops | bytes accessed | tf_op | source)
XLA Modules:
  0.0 697.5 jit_solution(16327532529719816883)
XLA Ops:
  7.9 4.9 collective-permute-start
  12.8 5.1 collective-permute-start.1
  18.0 1.7 fusion.28
  19.7 1.7 fusion.27
  21.4 1.9 fusion.26
  28.8 54.8 %gather_fusion = f32[16384,8]{1,0:T(8,128)} fusion(f32[8,4352]{0,1:T(8,128)S(1)} %copy.43, s32[16384]{0:T(1024)S(1)} %broadcast_clamp_fusion), kind=kCustom, calls=%fused_computation | custom fusion | bytes 1114112 | tf_op jit(solution)/shard_map/gather | solution.py:31
  83.6 5.5 copy.44
  91.7 4.6 copy.63
  96.3 88.2 %scatter_custom_fusion = f32[8,4352]{0,1:T(8,128)S(1)} fusion(s32[16384]{0:T(1024)S(1)} %bitcast.108, f32[16384,8]{1,0:T(8,128)} %bitcast.104, f32[]{:T(128)} %constant.95.clone.1), kind=kCustom, calls=%fused_computation.3 | custom fusion | flops 131072 | bytes 139776 | tf_op jit(solution)/shard_map/scatter-add | solution.py:47
  185.9 2.2 copy.64
  188.2 1.9 collective-permute-start.2
  190.2 3.7 collective-permute-start.3
  195.9 62.5 %all-gather.2.cloned.1.call-done = f32[128,4096]{1,0:T(8,128)} async-done(((f32[8,4096]{1,0:T(8,128)}), f32[128,4096]{1,0:T(8,128)}) %all-gather.2.cloned.1.call-update) | async-done | bytes 2097168 | tf_op jit(solution)/shard_map/all_gather | solution.py:82
  258.5 4.7 fusion.32
  263.4 187.4 %all-reduce.3.cloned.1.call-done = f32[128,128]{0,1:T(8,128)} async-done(((f32[128,128]{0,1:T(8,128)}), f32[128,128]{0,1:T(8,128)}) %all-reduce.3.cloned.1.call-update) | async-done | bytes 65552 | tf_op jit(solution)/shard_map/psum | solution.py:51
  452.6 11.7 %cholesky.44 = f32[128,128]{1,0:T(8,128)S(1)} custom-call(f32[128,128]{1,0:T(8,128)S(1)} %fusion.8), custom_call_target="Cholesky" | custom-call | tf_op jit(solution)/shard_map/jit(cholesky)/cholesky | solution.py:58
  465.7 9.8 %custom-call.6 = f32[1,128,128]{1,2,0:T(8,128)S(1)} custom-call(f32[1,128,128]{2,1,0:T(8,128)S(1)} %fusion.12), custom_call_target="InvertDiagBlocksLowerTriangular" | custom-call | tf_op jit(solution)/shard_map/triangular_solve/custom-call.0 | solution.py:59
  475.5 3.5 fusion.6
  479.0 2.4 fusion.33
  481.5 179.9 %all-reduce.5.cloned.1.call-done = f32[128,128]{0,1:T(8,128)} async-done(((f32[128,128]{0,1:T(8,128)}), f32[128,128]{0,1:T(8,128)}) %all-reduce.5.cloned.1.call-update) | async-done | bytes 65552 | tf_op jit(solution)/shard_map/psum | solution.py:51
  663.2 11.9 %cholesky.55 = f32[128,128]{1,0:T(8,128)S(1)} custom-call(f32[128,128]{1,0:T(8,128)S(1)} %fusion.5), custom_call_target="Cholesky" | custom-call | tf_op jit(solution)/shard_map/jit(cholesky)/cholesky | solution.py:63
  675.8 2.1 convolution_multiply_fusion
  678.5 9.8 %custom-call.7 = f32[1,128,128]{1,2,0:T(8,128)S(1)} custom-call(f32[1,128,128]{2,1,0:T(8,128)S(1)} %select_bitcast_fusion), custom_call_target="InvertDiagBlocksLowerTriangular" | custom-call | tf_op jit(solution)/shard_map/triangular_solve/custom-call.0 | solution.py:64
  688.3 1.9 fusion.3
  (60 shorter events, 19.5 us)
Async XLA Ops:
  7.2 251.3 %all-gather.2.cloned.1.call-start = ((), (), s32[]{:S(2)}) async-start(), calls=%async_computation | async-start | bytes 2228224 | tf_op jit(solution)/shard_map/all_gather | solution.py:82
  7.9 19.3 %collective-permute-start = (f32[8,128]{1,0:T(8,128)S(1)}, f32[8,128]{1,0:T(8,128)S(1)}, u32[]{:S(2)}, u32[]{:S(2)}) collective-permute-start(f32[8,128]{1,0:T(8,128)S(1)} %get-tuple-element.103), channel_id=1, source_target_pairs={{0,1},{1,2},{2,3},{3,4},{4,5},{5,6},{6,7},{7,8},{8,9},{9,10},{10,1... | collective-permute-start | bytes 12296 | tf_op jit(solution)/shard_map/ppermute | solution.py:16
  12.8 14.4 %collective-permute-start.1 = (f32[8,128]{1,0:T(8,128)S(1)}, f32[8,128]{1,0:T(8,128)S(1)}, u32[]{:S(2)}, u32[]{:S(2)}) collective-permute-start(f32[8,128]{1,0:T(8,128)S(1)} %get-tuple-element.104), channel_id=1, source_target_pairs={{1,0},{2,1},{3,2},{4,3},{5,4},{6,5},{7,6},{8,7},{9,8},{10,9},{11,1... | collective-permute-start | bytes 12296 | tf_op jit(solution)/shard_map/ppermute | solution.py:19
  185.9 7.9 %copy-start = (f32[8,4096]{1,0:T(8,128)S(1)}, f32[8,4096]{1,0:T(8,128)}, u32[]{:S(2)}) copy-start(f32[8,4096]{1,0:T(8,128)} %param.12) | copy-start | bytes 393220
  185.9 7.9 %copy-start.2 = (f32[4096]{0:T(1024)S(1)}, f32[4096]{0:T(1024)}, u32[]{:S(2)}) copy-start(f32[4096]{0:T(1024)} %param.15) | copy-start | bytes 49156
  188.2 5.7 collective-permute-start.2
  190.2 4.4 collective-permute-start.3
  195.2 0.7 copy-start.1
  195.9 255.0 %all-reduce.3.cloned.1.call-start = ((), (), s32[]{:S(2)}) async-start(), calls=%async_computation.1 | async-start | bytes 131072 | tf_op jit(solution)/shard_map/psum | solution.py:51
  263.2 398.2 %all-reduce.5.cloned.1.call-start = ((), (), s32[]{:S(2)}) async-start(), calls=%async_computation.2 | async-start | bytes 131072 | tf_op jit(solution)/shard_map/psum | solution.py:51
Sparse Core Ops, SparseCore 0:
  196.0 62.4 all-gather.1
  263.3 187.4 all-reduce.2
  481.6 179.7 all-reduce.4
where the time goes:
time: 698 us; the launch traced here: 697 us
  waiting for transfers between devices  431 us (62%)
  other arithmetic  141 us (20%)
  local copies, waits for them, and re-layouts  81.6 us (12%)
  starting transfers between devices  15.9 us (2%)
  matrix products  14.7 us (2%)
  between operations  14.1 us (2%)
    psum x2, waiting for transfers between devices, gram_over_space(): return lax.psum(partial_value, 'space')  367 us
    scatter-add x1, other arithmetic, element_images(): return jnp.zeros(extended.shape, jnp.float32).at[:, local].add(pulled)  88.2 us
    all_gather x1, waiting for transfers between devices, on_device(): whole = lax.all_gather(images, 'probe', axis=0, tiled=True)  62.5 us
    gather x2, local copies, waits for them, and re-layouts, element_images(): gathered = extended[:, local]  60.3 us
  transfers between devices with their start and end apart: 7, of which 4 were waited for; matrix products, arithmetic and copies ran while one was open for 1% of the time, Pallas kernels for 0%

commit v1 on v0

--- a/solution.py
+++ b/solution.py
@@ -48,7 +48,7 @@
 
 
 def gram_over_space(partial_value):
-    return lax.psum(partial_value, "space")
+    return jnp.sum(lax.all_gather(partial_value, "space"), axis=0)
 
 
 def orthonormal(rows, reduce_gram):

time: 698 us -> 472 us (0.68)
  waiting for transfers between devices: 431 us -> 205 us
    psum x2 -> x0, waiting for transfers between devices: 367 us -> none  [gram_over_space(): return lax.psum(partial_value, 'space')]
    all_gather x0 -> x2, waiting for transfers between devices: none -> 141 us  [gram_over_space(): return jnp.sum(lax.all_gather(partial_value, 'space'), axis=0)]
  transfers between devices with their start and end apart: 7 -> 7, of which waited for: 4 -> 4; matrix products, arithmetic and copies ran while one was open for 1% -> 2% of each run, Pallas kernels for 0% -> 0%
where the time goes in v1:
time: 472 us
  waiting for transfers between devices  205 us (43%)
  other arithmetic  142 us (30%)
  local copies, waits for them, and re-layouts  79.9 us (17%)
  starting transfers between devices  15.9 us (3%)
  matrix products  14.6 us (3%)
  between operations  14.1 us (3%)
    all_gather x2, waiting for transfers between devices, gram_over_space(): return jnp.sum(lax.all_gather(partial_value, 'space'), axis=0)  141 us
    scatter-add x1, other arithmetic, element_images(): return jnp.zeros(extended.shape, jnp.float32).at[:, local].add(pulled)  88.2 us
    all_gather x1, waiting for transfers between devices, on_device(): whole = lax.all_gather(images, 'probe', axis=0, tiled=True)  62.5 us
    gather x2, local copies, waits for them, and re-layouts, element_images(): gathered = extended[:, local]  60.3 us
    another operation x3, other arithmetic, orthonormal(): lower_second = jnp.linalg.cholesky(gram_second)  12.6 us
    another operation x3, other arithmetic, orthonormal(): lower_first = jnp.linalg.cholesky(gram_first)  12.4 us
    another operation x2, other arithmetic, orthonormal(): lax.linalg.triangular_solve(lower_first, rows, left_side=True, lower=True)  10.5 us
    another operation x2, other arithmetic, orthonormal(): lax.linalg.triangular_solve(lower_second, basis_first, left_side=True, lo...  10.4 us
  transfers between devices with their start and end apart: 7, of which 4 were waited for; matrix products, arithmetic and copies ran while one was open for 2% of the time, Pallas kernels for 0%

profile of v1, /device:TPU:1, one launch (start us, length us, event | category | flops | bytes accessed | tf_op | source)
XLA Modules:
  0.0 471.5 jit_solution(9732390869500762336)
XLA Ops:
  7.9 4.9 %collective-permute-start = (f32[8,128]{1,0:T(8,128)S(1)}, f32[8,128]{1,0:T(8,128)S(1)}, u32[]{:S(2)}, u32[]{:S(2)}) collective-permute-start(f32[8,128]{1,0:T(8,128)S(1)} %get-tuple-element.103), channel_id=1, source_target_pairs={{0,1},{1,2},{2,3},{3,4},{4,5},{5,6},{6,7},{7,8},{8,9},{9,10},{10,1... | collective-permute-start | bytes 12296 | tf_op jit(solution)/shard_map/ppermute | solution.py:16
  12.8 5.1 %collective-permute-start.1 = (f32[8,128]{1,0:T(8,128)S(1)}, f32[8,128]{1,0:T(8,128)S(1)}, u32[]{:S(2)}, u32[]{:S(2)}) collective-permute-start(f32[8,128]{1,0:T(8,128)S(1)} %get-tuple-element.104), channel_id=1, source_target_pairs={{1,0},{2,1},{3,2},{4,3},{5,4},{6,5},{7,6},{8,7},{9,8},{10,9},{11,1... | collective-permute-start | bytes 12296 | tf_op jit(solution)/shard_map/ppermute | solution.py:19
  18.0 1.7 fusion.28
  21.4 1.9 fusion.26
  28.8 54.8 %gather_fusion = f32[16384,8]{1,0:T(8,128)} fusion(f32[8,4352]{0,1:T(8,128)S(1)} %copy.37, s32[16384]{0:T(1024)S(1)} %broadcast_clamp_fusion), kind=kCustom, calls=%fused_computation | custom fusion | bytes 1114112 | tf_op jit(solution)/shard_map/gather | solution.py:31
  83.6 5.5 %copy.38 = f32[16384,8]{0,1:T(8,128)S(1)} copy(f32[16384,8]{1,0:T(8,128)} %gather_fusion) | data formatting | bytes 1048576 | tf_op jit(solution)/shard_map/gather | solution.py:31
  91.7 4.6 copy.53
  96.3 88.2 %scatter_custom_fusion = f32[8,4352]{0,1:T(8,128)S(1)} fusion(s32[16384]{0:T(1024)S(1)} %bitcast.112, f32[16384,8]{1,0:T(8,128)} %bitcast.106, f32[]{:T(128)} %constant.96.clone.1), kind=kCustom, calls=%fused_computation.3 | custom fusion | flops 131072 | bytes 139776 | tf_op jit(solution)/shard_map/scatter-add | solution.py:47
  185.9 2.2 copy.54
  188.2 1.9 collective-permute-start.2
  190.2 3.7 collective-permute-start.3
  195.9 62.5 %all-gather.6.cloned.1.call-done = f32[128,4096]{1,0:T(8,128)} async-done(((f32[8,4096]{1,0:T(8,128)}), f32[128,4096]{1,0:T(8,128)}) %all-gather.6.cloned.1.call-update) | async-done | bytes 2097168 | tf_op jit(solution)/shard_map/all_gather | solution.py:82
  258.5 4.7 fusion.32
  263.4 72.8 %all-gather.8.cloned.1.call-done = f32[4096,128]{1,0:T(8,128)} async-done(((f32[128,128]{1,0:T(8,128)}), f32[4096,128]{1,0:T(8,128)}) %all-gather.8.cloned.1.call-update) | async-done | bytes 2097168 | tf_op jit(solution)/shard_map/all_gather | solution.py:51
  336.2 1.7 reduce_sum.18
  338.0 11.7 %cholesky.44 = f32[128,128]{1,0:T(8,128)S(1)} custom-call(f32[128,128]{1,0:T(8,128)S(1)} %fusion.8), custom_call_target="Cholesky" | custom-call | tf_op jit(solution)/shard_map/jit(cholesky)/cholesky | solution.py:58
  351.1 9.8 %custom-call.6 = f32[1,128,128]{1,2,0:T(8,128)S(1)} custom-call(f32[1,128,128]{2,1,0:T(8,128)S(1)} %fusion.12), custom_call_target="InvertDiagBlocksLowerTriangular" | custom-call | tf_op jit(solution)/shard_map/triangular_solve/custom-call.0 | solution.py:59
  360.9 3.5 fusion.6
  364.4 2.4 fusion.33
  366.8 68.6 %all-gather.10.cloned.1.call-done = f32[4096,128]{1,0:T(8,128)} async-done(((f32[128,128]{1,0:T(8,128)}), f32[4096,128]{1,0:T(8,128)}) %all-gather.10.cloned.1.call-update) | async-done | bytes 2097168 | tf_op jit(solution)/shard_map/all_gather | solution.py:51
  437.2 11.9 %cholesky.55 = f32[128,128]{1,0:T(8,128)S(1)} custom-call(f32[128,128]{1,0:T(8,128)S(1)} %fusion.5), custom_call_target="Cholesky" | custom-call | tf_op jit(solution)/shard_map/jit(cholesky)/cholesky | solution.py:63
  449.8 2.1 convolution_multiply_fusion
  452.5 9.8 %custom-call.7 = f32[1,128,128]{1,2,0:T(8,128)S(1)} custom-call(f32[1,128,128]{2,1,0:T(8,128)S(1)} %select_bitcast_fusion), custom_call_target="InvertDiagBlocksLowerTriangular" | custom-call | tf_op jit(solution)/shard_map/triangular_solve/custom-call.0 | solution.py:64
  462.4 1.9 fusion.3
  (62 shorter events, 19.5 us)
Async XLA Ops:
  7.2 251.3 %all-gather.6.cloned.1.call-start = ((), (), s32[]{:S(2)}) async-start(), calls=%async_computation | async-start | bytes 2228224 | tf_op jit(solution)/shard_map/all_gather | solution.py:82
  7.9 19.3 %collective-permute-start = (f32[8,128]{1,0:T(8,128)S(1)}, f32[8,128]{1,0:T(8,128)S(1)}, u32[]{:S(2)}, u32[]{:S(2)}) collective-permute-start(f32[8,128]{1,0:T(8,128)S(1)} %get-tuple-element.103), channel_id=1, source_target_pairs={{0,1},{1,2},{2,3},{3,4},{4,5},{5,6},{6,7},{7,8},{8,9},{9,10},{10,1... | collective-permute-start | bytes 12296 | tf_op jit(solution)/shard_map/ppermute | solution.py:16
  12.8 14.4 %collective-permute-start.1 = (f32[8,128]{1,0:T(8,128)S(1)}, f32[8,128]{1,0:T(8,128)S(1)}, u32[]{:S(2)}, u32[]{:S(2)}) collective-permute-start(f32[8,128]{1,0:T(8,128)S(1)} %get-tuple-element.104), channel_id=1, source_target_pairs={{1,0},{2,1},{3,2},{4,3},{5,4},{6,5},{7,6},{8,7},{9,8},{10,9},{11,1... | collective-permute-start | bytes 12296 | tf_op jit(solution)/shard_map/ppermute | solution.py:19
  185.9 7.9 %copy-start = (f32[8,4096]{1,0:T(8,128)S(1)}, f32[8,4096]{1,0:T(8,128)}, u32[]{:S(2)}) copy-start(f32[8,4096]{1,0:T(8,128)} %param.12) | copy-start | bytes 393220
  185.9 7.9 %copy-start.2 = (f32[4096]{0:T(1024)S(1)}, f32[4096]{0:T(1024)}, u32[]{:S(2)}) copy-start(f32[4096]{0:T(1024)} %param.15) | copy-start | bytes 49156
  188.2 5.7 %collective-permute-start.2 = (f32[8,128]{1,0:T(8,128)S(1)}, f32[8,128]{1,0:T(8,128)S(1)}, u32[]{:S(2)}, u32[]{:S(2)}) collective-permute-start(f32[8,128]{1,0:T(8,128)S(1)} %copy.55), channel_id=1, source_target_pairs={{1,0},{2,1},{3,2},{4,3},{5,4},{6,5},{7,6},{8,7},{9,8},{10,9},{11,1... | collective-permute-start | bytes 12296 | tf_op jit(solution)/shard_map/ppermute | solution.py:27
  190.2 4.4 collective-permute-start.3
  195.2 0.7 copy-start.1
  195.9 140.3 %all-gather.8.cloned.1.call-start = ((), (), s32[]{:S(2)}) async-start(), calls=%async_computation.1 | async-start | bytes 2162688 | tf_op jit(solution)/shard_map/all_gather | solution.py:51
  263.2 172.2 %all-gather.10.cloned.1.call-start = ((), (), s32[]{:S(2)}) async-start(), calls=%async_computation.2 | async-start | bytes 2162688 | tf_op jit(solution)/shard_map/all_gather | solution.py:51
Sparse Core Ops, SparseCore 0:
  196.0 62.4 all-gather.5
  263.3 72.8 all-gather.7
  366.9 68.4 all-gather.9
